TPU v7x, 256 devices: a whole 4x4x8 slice. The times are simulated.
256 devices in a mesh: inp: 2 (over y_hi), pa: 16 (over x, y_lo, core), pb: 8 (over z).
Axes of the slice: x: 4, y: 4 (y_hi: 2, y_lo: 2; y = y_hi * 2 + y_lo), z: 8, core: 2. Of those that a mesh axis runs over, the one named last changes fastest.
Arguments:
- log_inputs: float32 [2, 256, 256, 256], P('inp', 'pa', 'pb'), may hold values from -6 to 6
- warm_potential: float32 [2, 256, 256, 256], P('inp', 'pa', 'pb'), may hold values from -6 to 6
- bary_weights: float32 [2], P('inp'), may hold values from 0.1 to 0.5
- band_reach: int32 [3], replicated, may hold values from 0 to 2, each once
- bary_cotangent: float32 [256, 256, 256], P('pa', 'pb', 'inp'), may hold values from -6 to 6
Outputs:
- barycenter: float32 [256, 256, 256], P('pa', 'pb', 'inp')
- input_grad: float32 [2, 256, 256, 256], P('inp', 'pa', 'pb')
Inputs may be any that keep to these rules, and one draw needn't show every extreme that they name: `band_reach`: a permutation of 0, 1 and 2, one entry a line direction.
All inputs are finite; a program needn't handle non-finite values.
Results may differ from a plain program's by a relative error of at most 0.00022.
Values sent between devices are 32-bit elements; how exact they have to be, the bound alone decides.
A program may use at most 64 MiB of HBM per device.

v0:
```python
import math

import jax
import jax.numpy as jnp
from jax import lax
from jax.sharding import PartitionSpec as P

FORMS = ("ij,kjbc->kibc", "ij,kajc->kaic", "ij,kabj->kabi")


def line_kernel(length, reach):
    index = jnp.arange(length, dtype=jnp.int32)
    block = 4
    sigma = 3.0
    offset = (index[:, None] - index[None, :]).astype(jnp.float32)
    inside = jnp.abs(index[:, None] // block - index[None, :] // block) <= reach
    gauss = jnp.exp(-offset * offset / (2.0 * sigma * sigma)) / (sigma * math.sqrt(2.0 * math.pi))
    return 0.5 * jnp.eye(length, dtype=jnp.float32) + 0.5 * jnp.where(
        inside, gauss, jnp.zeros_like(gauss)
    )


def along_line(kernel, field, line):
    return jnp.einsum(
        FORMS[line],
        kernel,
        field,
        precision=lax.Precision.HIGHEST,
        preferred_element_type=jnp.float32,
    )


def move_once(field, source, target):
    if source == 0:
        return lax.all_to_all(field, "pa", split_axis=1, concat_axis=2, tiled=True)
    if source == 2:
        return lax.all_to_all(field, "pb", split_axis=3, concat_axis=2, tiled=True)
    if target == 2:
        return lax.all_to_all(field, "pb", split_axis=2, concat_axis=3, tiled=True)
    return lax.all_to_all(field, "pa", split_axis=2, concat_axis=1, tiled=True)


def relayout(field, source, target):
    for turn in range(abs(target - source)):
        following = source + (1 if target > source else -1)
        field = move_once(field, source, following)
        source = following
    return field


def log_conv(field, kernels, order, start, home):
    stored = []
    layout = start
    value = field
    for line in order:
        value = relayout(value, layout, line)
        layout = line
        result = jnp.log(along_line(kernels[line], jnp.exp(value), line))
        stored.append((value, result, line))
        value = result
    return (relayout(value, layout, home), stored)


def conv_adjoint(cotangent, stored, kernels, layout):
    for value, result, line in reversed(stored):
        cotangent = relayout(cotangent, layout, line)
        layout = line
        cotangent = jnp.exp(value) * along_line(kernels[line], cotangent * jnp.exp(-result), line)
    return (cotangent, layout)


def per_device(log_inputs, warm_potential, bary_weights, band_reach, bary_cotangent):
    length = log_inputs.shape[3]
    kernels = [line_kernel(length, band_reach[line]) for line in range(3)]
    weights = bary_weights[:, None, None, None]
    first_order = (0, 1, 2)
    first_home = 2
    second_order = (0, 1, 2)
    inputs_there = relayout(log_inputs, 2, first_home)
    image_one, unused_one = log_conv(warm_potential, kernels, first_order, 2, first_home)
    dual_one = inputs_there - image_one
    image_two, stored_two = log_conv(dual_one, kernels, second_order, first_home, 2)
    part_one = warm_potential + image_two
    barycenter = lax.psum_scatter(
        jnp.sum(weights * part_one, axis=0), "inp", scatter_dimension=2, tiled=True
    )
    cotangent = lax.all_gather(bary_cotangent, "inp", axis=2, tiled=True)
    one_bar = weights * cotangent[None]
    dual_one_bar, one_layout = conv_adjoint(one_bar, stored_two, kernels, 2)
    input_grad = relayout(dual_one_bar, one_layout, 2)
    return (barycenter, input_grad)


def solution(mesh):
    return jax.shard_map(
        per_device,
        mesh=mesh,
        in_specs=(
            P("inp", "pa", "pb", None),
            P("inp", "pa", "pb", None),
            P("inp"),
            P(),
            P("pa", "pb", "inp"),
        ),
        out_specs=(P("pa", "pb", "inp"), P("inp", "pa", "pb", None)),
        check_vma=False,
    )
```

profile of v0, /device:TPU:9, one launch (start us, length us, event | category | flops | bytes accessed | tf_op | source)
XLA Modules:
  0.0 386.5 jit_solution(17372530566642108212)
XLA Ops:
  10.4 24.1 %all_to_all.162 = f32[8,1,16384]{2,1,0:T(1,128)S(1)} all-to-all(f32[8,1,16384]{2,1,0:T(1,128)S(1)} %reshape.181), channel_id=1, replica_groups=mesh['inp'=2,'pa'=16,'pb'=8] {'pb'}, dimensions={0} | all-to-all | bytes 1048576 | tf_op jit(solution)/shard_map/all_to_all | solution.py:37
  40.1 3.1 reshape.183
  43.2 8.1 %all-to-all-start.1 = ((f32[16,1,8192]{2,1,0:T(1,128)}), f32[16,1,8192]{2,1,0:T(1,128)S(1)}, u32[]{:S(2)}, u32[]{:S(2)}) async-start(f32[16,1,8192]{2,1,0:T(1,128)} %reshape.183), calls=%async_computation.1 | async-start | bytes 1048576 | tf_op jit(solution)/shard_map/all_to_all | solution.py:40
  52.0 8.7 %all-to-all-done.1 = f32[16,1,8192]{2,1,0:T(1,128)S(1)} async-done(((f32[16,1,8192]{2,1,0:T(1,128)}), f32[16,1,8192]{2,1,0:T(1,128)S(1)}, u32[]{:S(2)}, u32[]{:S(2)}) %all-to-all-start.1) | async-done | bytes 524320 | tf_op jit(solution)/shard_map/all_to_all | solution.py:40
  68.9 14.0 %all_to_all.163 = f32[16,1,8192]{2,1,0:T(1,128)S(1)} all-to-all(f32[16,1,8192]{2,1,0:T(1,128)S(1)} %reshape.185), channel_id=1, replica_groups=mesh['inp'=2,'pa'=16,'pb'=8] {'pa'}, dimensions={0} | all-to-all | bytes 1048576 | tf_op jit(solution)/shard_map/all_to_all | solution.py:35
  86.0 4.2 %fusion.10 = f32[1,16,256,32]{2,3,1,0:T(8,128)S(1)} fusion(f32[16,256,32]{2,1,0:T(8,128)S(1)} %bitcast.203, s32[]{:T(128)} %bitcast.17, s32[256]{0:T(256)S(1)} %and_select_fusion), kind=kOutput, calls=%fused_computation.19 | convolution fusion | flops 403570688 | bytes 1049604 | tf_op jit(solution)/shard_map/ij,kajc->kaic/dot_general | solution.py:24
  92.4 20.6 %all_to_all.164 = f32[8,1,16384]{2,1,0:T(1,128)S(1)} all-to-all(f32[8,1,16384]{2,1,0:T(1,128)S(1)} %reshape.187), channel_id=1, replica_groups=mesh['inp'=2,'pa'=16,'pb'=8] {'pb'}, dimensions={0} | all-to-all | bytes 1048576 | tf_op jit(solution)/shard_map/all_to_all | solution.py:39
  122.3 20.3 %all_to_all.165 = f32[8,1,16384]{2,1,0:T(1,128)S(1)} all-to-all(f32[8,1,16384]{2,1,0:T(1,128)S(1)} %reshape.189), channel_id=1, replica_groups=mesh['inp'=2,'pa'=16,'pb'=8] {'pb'}, dimensions={0} | all-to-all | bytes 1048576 | tf_op jit(solution)/shard_map/all_to_all | solution.py:37
  150.0 13.6 %all_to_all.166 = f32[16,1,8192]{2,1,0:T(1,128)S(1)} all-to-all(f32[16,1,8192]{2,1,0:T(1,128)S(1)} %reshape.191), channel_id=1, replica_groups=mesh['inp'=2,'pa'=16,'pb'=8] {'pa'}, dimensions={0} | all-to-all | bytes 1048576 | tf_op jit(solution)/shard_map/all_to_all | solution.py:40
  167.1 4.4 %fusion.5 = f32[1,256,16,32]{1,3,2,0:T(8,128)S(1)} fusion(f32[256,16,32]{2,1,0:T(8,128)S(1)} %bitcast.172, s32[]{:T(128)} %bitcast.1, s32[256]{0:T(256)S(1)} %and_select_fusion), kind=kOutput, calls=%fused_computation.10 | convolution fusion | flops 403570688 | bytes 1049604 | tf_op jit(solution)/shard_map/ij,kjbc->kibc/dot_general | solution.py:24
  176.5 14.3 %all_to_all.167 = f32[16,1,8192]{2,1,0:T(1,128)} all-to-all(f32[16,1,8192]{2,1,0:T(1,128)S(1)} %reshape.193), channel_id=1, replica_groups=mesh['inp'=2,'pa'=16,'pb'=8] {'pa'}, dimensions={0} | all-to-all | bytes 1048576 | tf_op jit(solution)/shard_map/all_to_all | solution.py:35
  199.2 4.2 %fusion.8 = f32[1,16,256,32]{2,3,1,0:T(8,128)S(1)} fusion(f32[16,256,32]{2,1,0:T(8,128)S(1)} %bitcast.174, s32[]{:T(128)} %bitcast.17, s32[256]{0:T(256)S(1)} %and_select_fusion), kind=kOutput, calls=%fused_computation.15 | convolution fusion | flops 403570688 | bytes 1049604 | tf_op jit(solution)/shard_map/ij,kajc->kaic/dot_general | solution.py:24
  205.8 3.1 reshape.195
  209.0 4.1 %all-to-all-start.7 = ((f32[8,1,16384]{2,1,0:T(1,128)}), f32[8,1,16384]{2,1,0:T(1,128)}, u32[]{:S(2)}, u32[]{:S(2)}) async-start(f32[8,1,16384]{2,1,0:T(1,128)} %reshape.195), calls=%async_computation.7 | async-start | bytes 1048576 | tf_op jit(solution)/shard_map/all_to_all | solution.py:39
  213.8 10.5 %all_gather.3 = f32[16,32,256]{2,1,0:T(8,128)} all-gather(f32[16,32,128]{2,1,0:T(8,128)S(1)} %copy-done.5), channel_id=1, replica_groups=mesh['inp'=2,'pa'=16,'pb'=8] {'inp'}, dimensions={2}, use_global_device_ids=true | all-gather | bytes 786432 | tf_op jit(solution)/shard_map/all_gather | solution.py:87
  224.3 6.9 %all-to-all-done.7 = f32[8,1,16384]{2,1,0:T(1,128)} async-done(((f32[8,1,16384]{2,1,0:T(1,128)}), f32[8,1,16384]{2,1,0:T(1,128)}, u32[]{:S(2)}, u32[]{:S(2)}) %all-to-all-start.7) | async-done | bytes 524320 | tf_op jit(solution)/shard_map/all_to_all | solution.py:39
  231.2 3.7 reduce.7
  248.3 3.4 fusion.13
  251.7 3.5 copy.95
  255.2 3.1 reshape.197
  258.3 4.3 %all-to-all-start.8 = ((f32[8,1,16384]{2,1,0:T(1,128)}), f32[8,1,16384]{2,1,0:T(1,128)}, u32[]{:S(2)}, u32[]{:S(2)}) async-start(f32[8,1,16384]{2,1,0:T(1,128)} %reshape.197), calls=%async_computation.9 | async-start | bytes 1048576 | tf_op jit(solution)/shard_map/all_to_all | solution.py:37
  265.6 15.0 %all-to-all-done.8 = f32[8,1,16384]{2,1,0:T(1,128)} async-done(((f32[8,1,16384]{2,1,0:T(1,128)}), f32[8,1,16384]{2,1,0:T(1,128)}, u32[]{:S(2)}, u32[]{:S(2)}) %all-to-all-start.8) | async-done | bytes 524320 | tf_op jit(solution)/shard_map/all_to_all | solution.py:37
  280.6 3.7 reduce.8
  287.4 4.1 %copy.127 = f32[1,16,32,8,32]{2,3,4,1,0:T(8,128)} copy(f32[1,16,32,8,32]{2,1,4,3,0:T(8,128)} %bitcast.194) | data formatting | bytes 1048576 | tf_op jit(solution)/shard_map/all_to_all | solution.py:37
  294.2 3.4 fusion.11
  297.7 3.5 copy.98
  304.3 4.4 %all-to-all-start.9 = ((f32[16,1,8192]{2,1,0:T(1,128)}), f32[16,1,8192]{2,1,0:T(1,128)}, u32[]{:S(2)}, u32[]{:S(2)}) async-start(f32[16,1,8192]{2,1,0:T(1,128)} %reshape.199), calls=%async_computation.10 | async-start | bytes 1048576 | tf_op jit(solution)/shard_map/all_to_all | solution.py:40
  310.5 7.6 %all-to-all-done.9 = f32[16,1,8192]{2,1,0:T(1,128)} async-done(((f32[16,1,8192]{2,1,0:T(1,128)}), f32[16,1,8192]{2,1,0:T(1,128)}, u32[]{:S(2)}, u32[]{:S(2)}) %all-to-all-start.9) | async-done | bytes 524320 | tf_op jit(solution)/shard_map/all_to_all | solution.py:40
  324.5 3.2 fusion.12
  331.8 4.8 %all-to-all-start.10 = ((f32[16,1,8192]{2,1,0:T(1,128)}), f32[16,1,8192]{2,1,0:T(1,128)S(1)}, u32[]{:S(2)}, u32[]{:S(2)}) async-start(f32[16,1,8192]{2,1,0:T(1,128)} %reshape.201), calls=%async_computation.11 | async-start | bytes 1048576 | tf_op jit(solution)/shard_map/all_to_all | solution.py:35
  337.8 8.3 %all-to-all-done.10 = f32[16,1,8192]{2,1,0:T(1,128)S(1)} async-done(((f32[16,1,8192]{2,1,0:T(1,128)}), f32[16,1,8192]{2,1,0:T(1,128)S(1)}, u32[]{:S(2)}, u32[]{:S(2)}) %all-to-all-start.10) | async-done | bytes 524320 | tf_op jit(solution)/shard_map/all_to_all | solution.py:35
  351.0 20.4 %all_to_all.168 = f32[8,1,16384]{2,1,0:T(1,128)S(1)} all-to-all(f32[8,1,16384]{2,1,0:T(1,128)S(1)} %reshape.203), channel_id=1, replica_groups=mesh['inp'=2,'pa'=16,'pb'=8] {'pb'}, dimensions={0} | all-to-all | bytes 1048576 | tf_op jit(solution)/shard_map/all_to_all | solution.py:39
  (91 shorter events, 110.3 us)
Async XLA Ops:
  40.0 11.3 %copy-start.6 = (s32[3]{0:T(128)S(1)}, s32[3]{0:T(128)}, u32[]{:S(2)}) copy-start(s32[3]{0:T(128)} %param.8) | copy-start | bytes 40
  43.2 17.5 %all-to-all-start.1 = ((f32[16,1,8192]{2,1,0:T(1,128)}), f32[16,1,8192]{2,1,0:T(1,128)S(1)}, u32[]{:S(2)}, u32[]{:S(2)}) async-start(f32[16,1,8192]{2,1,0:T(1,128)} %reshape.183), calls=%async_computation.1 | async-start | bytes 1048576 | tf_op jit(solution)/shard_map/all_to_all | solution.py:40
  197.9 1.4 copy-start
  205.8 7.9 %copy-start.5 = (f32[16,32,128]{2,1,0:T(8,128)S(1)}, f32[16,32,128]{2,1,0:T(8,128)}, u32[]{:S(2)}) copy-start(f32[16,32,128]{2,1,0:T(8,128)} %param.9) | copy-start | bytes 786436
  209.0 22.2 %all-to-all-start.7 = ((f32[8,1,16384]{2,1,0:T(1,128)}), f32[8,1,16384]{2,1,0:T(1,128)}, u32[]{:S(2)}, u32[]{:S(2)}) async-start(f32[8,1,16384]{2,1,0:T(1,128)} %reshape.195), calls=%async_computation.7 | async-start | bytes 1048576 | tf_op jit(solution)/shard_map/all_to_all | solution.py:39
  247.5 0.8 copy-start.2
  258.3 22.3 %all-to-all-start.8 = ((f32[8,1,16384]{2,1,0:T(1,128)}), f32[8,1,16384]{2,1,0:T(1,128)}, u32[]{:S(2)}, u32[]{:S(2)}) async-start(f32[8,1,16384]{2,1,0:T(1,128)} %reshape.197), calls=%async_computation.9 | async-start | bytes 1048576 | tf_op jit(solution)/shard_map/all_to_all | solution.py:37
  304.3 13.8 %all-to-all-start.9 = ((f32[16,1,8192]{2,1,0:T(1,128)}), f32[16,1,8192]{2,1,0:T(1,128)}, u32[]{:S(2)}, u32[]{:S(2)}) async-start(f32[16,1,8192]{2,1,0:T(1,128)} %reshape.199), calls=%async_computation.10 | async-start | bytes 1048576 | tf_op jit(solution)/shard_map/all_to_all | solution.py:40
  322.6 1.8 copy-start.4
  330.0 6.9 %copy-start.1 = (f32[1,16,32,256]{3,2,1,0:T(8,128)S(1)}, f32[1,16,32,256]{3,2,1,0:T(8,128)}, u32[]{:S(2)}) copy-start(f32[1,16,32,256]{3,2,1,0:T(8,128)} %param.6) | copy-start | bytes 1572868
  330.0 6.9 %copy-start.3 = (f32[16,32,256]{2,1,0:T(8,128)S(1)}, f32[16,32,256]{2,1,0:T(8,128)}, u32[]{:S(2)}) copy-start(f32[16,32,256]{2,1,0:T(8,128)} %copy-done.2) | copy-start | bytes 1572868
  331.8 14.3 %all-to-all-start.10 = ((f32[16,1,8192]{2,1,0:T(1,128)}), f32[16,1,8192]{2,1,0:T(1,128)S(1)}, u32[]{:S(2)}, u32[]{:S(2)}) async-start(f32[16,1,8192]{2,1,0:T(1,128)} %reshape.201), calls=%async_computation.11 | async-start | bytes 1048576 | tf_op jit(solution)/shard_map/all_to_all | solution.py:35
  336.6 42.8 %reduce-scatter.2.cloned.1.call-start = ((), (), s32[]{:S(2)}) async-start(), calls=%async_computation.13 | async-start | bytes 786432 | tf_op jit(solution)/shard_map/reduce_scatter | solution.py:84
Sparse Core Ops, SparseCore 0:
  340.5 15.9 reduce-scatter.1
where the time goes:
time: 393 us; the launch traced here: 387 us
  blocking collectives  138 us (35%)
  local copies, waits for them, and re-layouts  102 us (26%)
  waiting for transfers between devices  46.4 us (12%)
  other arithmetic  29.2 us (7%)
  matrix products  29.2 us (7%)
  starting transfers between devices  26.1 us (7%)
  between operations  15.5 us (4%)
    all_to_all x2, blocking collectives, move_once(): return lax.all_to_all(field, 'pb', split_axis=3, concat_axis=2, tiled=True)  44.4 us
    unnamed x39, local copies, waits for them, and re-layouts  42.4 us
    all_to_all x2, blocking collectives, move_once(): return lax.all_to_all(field, 'pb', split_axis=2, concat_axis=3, tiled=True)  41 us
    all_to_all x2, blocking collectives, move_once(): return lax.all_to_all(field, 'pa', split_axis=1, concat_axis=2, tiled=True)  28.3 us
    dot_general x8, matrix products, along_line(): jnp.einsum(FORMS[line], kernel, field, precision=lax.Precision.HIGHEST, p...  27.7 us
    exp x17, local copies, waits for them, and re-layouts, log_conv(): result = jnp.log(along_line(kernels[line], jnp.exp(value), line))  19.4 us
    all_to_all x2, waiting for transfers between devices, move_once(): return lax.all_to_all(field, 'pa', split_axis=2, concat_axis=1, tiled=True)  16.3 us
    all_to_all x1, waiting for transfers between devices, move_once(): return lax.all_to_all(field, 'pb', split_axis=3, concat_axis=2, tiled=True)  15 us
  transfers between devices with their start and end apart: 6, of which 5 were waited for; matrix products, arithmetic and copies ran while one was open for 5% of the time, Pallas kernels for 0%

commit v1 on v0

v1 whole, which is shorter than its diff:
```python
import functools
import math

import jax
import jax.numpy as jnp
from jax import lax
from jax.experimental import pallas as pl
from jax.experimental.pallas import tpu as pltpu
from jax.sharding import PartitionSpec as P

MESH = pl.DeviceIdType.MESH
F32 = jnp.float32
BF16 = jnp.bfloat16
BLOCK = 4
SIGMA = 3.0
TILE = 8
ORDER = (1, 2, 0, 3)


def weight(row, column, reach):
    offset = (row - column).astype(F32)
    inside = jnp.abs(row // BLOCK - column // BLOCK) <= reach
    gauss = jnp.exp(-offset * offset / (2.0 * SIGMA * SIGMA)) / (SIGMA * math.sqrt(2.0 * math.pi))
    return 0.5 * jnp.where(row == column, 1.0, 0.0) + 0.5 * jnp.where(inside, gauss, 0.0)


def iotas(rows, columns):
    shape = (rows, columns)
    return lax.broadcasted_iota(jnp.int32, shape, 0), lax.broadcasted_iota(jnp.int32, shape, 1)


def split(value):
    high = value.astype(BF16)
    return high, (value - high.astype(F32)).astype(BF16)


def dot(a, b):
    return jnp.dot(a, b, preferred_element_type=F32)


def kernel(
    rx, ry, reach_ref, w_ref, warm_hbm, log_hbm, cot_hbm, bary_hbm, grad_hbm,
    warm_v, log_v, u, v, cot_v, part_v, peer_v, bary_v, grad_v,
    mxh, mxl, myh, myl, kzh, kzl,
    in_sem, out_sem, x_send, x_recv, y_send, y_recv, i_send, i_recv,
):
    hx = BLOCK * rx
    inp, pa, pb = (lax.axis_index(name) for name in ("inp", "pa", "pb"))
    last_a, last_b = lax.axis_size("pa") - 1, lax.axis_size("pb") - 1
    has = {
        ("x", 0): pa > 0, ("x", 1): pa < last_a,
        ("y", 0): pb > 0, ("y", 1): pb < last_b,
    }
    near = {
        ("x", 0): {"pa": pa - 1}, ("x", 1): {"pa": pa + 1},
        ("y", 0): {"pb": pb - 1}, ("y", 1): {"pb": pb + 1},
    }
    partner = {"inp": 1 - inp}

    loads = [
        pltpu.make_async_copy(warm_hbm, warm_v, in_sem.at[0]),
        pltpu.make_async_copy(log_hbm, log_v, in_sem.at[1]),
        pltpu.make_async_copy(cot_hbm, cot_v.at[inp], in_sem.at[2]),
    ]
    for load in loads:
        load.start()

    barrier = pltpu.get_barrier_semaphore()
    pl.semaphore_signal(barrier, inc=1, device_id=partner, device_id_type=MESH)
    for key, there in has.items():
        @pl.when(there)
        def _(key=key):
            pl.semaphore_signal(barrier, inc=1, device_id=near[key], device_id_type=MESH)

    row, column = iotas(*mxh.shape)
    entries = weight(row // TILE + hx, column // TILE, reach_ref[0])
    mxh[...], mxl[...] = split(jnp.where(row % TILE == column % TILE, entries, 0.0))
    row, column = iotas(*myh.shape)
    lead = TILE if ry else 0
    entries = weight(row % TILE + lead, (column // 64) * TILE + column % TILE, reach_ref[1])
    mine = row // TILE == (column % 64) // TILE
    myh[...], myl[...] = split(jnp.where(mine, entries, 0.0))
    row, column = iotas(*kzh.shape)
    kzh[...], kzl[...] = split(weight(row, column, reach_ref[2]))

    if rx:
        for side, rows in ((0, pl.ds(0, hx)), (1, pl.ds(hx + 16, hx))):
            @pl.when(jnp.logical_not(has["x", side]))
            def _(rows=rows):
                for turn in range(3):
                    for g in range(4):
                        u[turn, g, rows] = jnp.zeros((hx, TILE, 256), F32)
    if ry:
        for side, g in ((0, 0), (1, 5)):
            @pl.when(jnp.logical_not(has["y", side]))
            def _(g=g):
                for turn in range(3):
                    v[turn, g] = jnp.zeros((16, TILE, 256), F32)

    own = pl.ds(hx, 16)

    def tile(ref, g):
        return ref[:, pl.ds(TILE * g, TILE), :]

    loads[0].wait()
    for g in ORDER:
        u[0, g, own] = jnp.exp(tile(warm_v, g))

    pl.semaphore_wait(barrier, 1 + sum(there.astype(jnp.int32) for there in has.values()))

    def x_copy(turn, g, side):
        source = u.at[turn, g, pl.ds(hx + (0 if side == 0 else 16 - hx), hx)]
        target = u.at[turn, g, pl.ds(hx + 16 if side == 0 else 0, hx)]
        return pltpu.make_async_remote_copy(
            src_ref=source, dst_ref=target,
            send_sem=x_send.at[turn, g, side], recv_sem=x_recv.at[turn, g, 1 - side],
            device_id=near["x", side], device_id_type=MESH,
        )

    def x_arrival(turn, g, side):
        target = u.at[turn, g, pl.ds(0 if side == 0 else hx + 16, hx)]
        return pltpu.make_async_remote_copy(
            src_ref=target, dst_ref=target,
            send_sem=x_send.at[turn, g, side], recv_sem=x_recv.at[turn, g, side],
            device_id=near["x", side], device_id_type=MESH,
        )

    def y_copy(turn, side):
        return pltpu.make_async_remote_copy(
            src_ref=v.at[turn, 1 if side == 0 else 4], dst_ref=v.at[turn, 5 if side == 0 else 0],
            send_sem=y_send.at[turn, side], recv_sem=y_recv.at[turn, 1 - side],
            device_id=near["y", side], device_id_type=MESH,
        )

    def y_arrival(turn, side):
        target = v.at[turn, 0 if side == 0 else 5]
        return pltpu.make_async_remote_copy(
            src_ref=target, dst_ref=target,
            send_sem=y_send.at[turn, side], recv_sem=y_recv.at[turn, side],
            device_id=near["y", side], device_id_type=MESH,
        )

    def peer_copy(which, source, target):
        return pltpu.make_async_remote_copy(
            src_ref=source, dst_ref=target, send_sem=i_send.at[which], recv_sem=i_recv.at[which],
            device_id=partner, device_id_type=MESH,
        )

    def x_start(turn, g):
        if rx:
            for side in (0, 1):
                @pl.when(has["x", side])
                def _(side=side):
                    x_copy(turn, g, side).start()

    def x_wait(turn, g):
        if rx:
            for side in (0, 1):
                @pl.when(has["x", side])
                def _(side=side):
                    x_arrival(turn, g, side).wait_recv()

    def y_start(turn, side):
        if ry:
            @pl.when(has["y", side])
            def _():
                y_copy(turn, side).start()

    def y_wait(turn, side):
        if ry:
            @pl.when(has["y", side])
            def _():
                y_arrival(turn, side).wait_recv()

    for g in ORDER:
        x_start(0, g)
    loads[2].wait()
    cot_copy = peer_copy(0, cot_v.at[inp], cot_v.at[inp])
    cot_copy.start()
    loads[1].wait()

    lead_y = 1 if ry else 0
    depth_y = 3 if ry else 1
    stores = []
    for turn in range(3):
        for g in ORDER:
            x_wait(turn, g)
            high, low = split(u[turn, g].reshape(-1, 256))
            done = dot(mxh[...], high) + dot(mxl[...], high) + dot(mxh[...], low)
            v[turn, g + lead_y] = done.reshape(16, TILE, 256)
            if g == 0:
                y_start(turn, 0)
            if g == 3:
                y_start(turn, 1)
        if turn == 1:
            peer_copy(0, cot_v.at[1 - inp], cot_v.at[1 - inp]).wait_recv()
        for g in ORDER:
            if g == 0:
                y_wait(turn, 0)
            if g == 3:
                y_wait(turn, 1)
            halves = []
            for half in (0, 1):
                piece = v[turn, pl.ds(g, depth_y), pl.ds(8 * half, 8)].reshape(-1, 256)
                high, low = split(piece)
                halves.append(dot(myh[...], high) + dot(myl[...], high) + dot(myh[...], low))
            high, low = split(jnp.concatenate(halves, axis=0))
            done = dot(high, kzh[...]) + dot(low, kzh[...]) + dot(high, kzl[...])
            done = done.reshape(16, TILE, 256)
            if turn == 0:
                u[1, g, own] = jnp.exp(tile(log_v, g)) / done
                x_start(1, g)
            elif turn == 1:
                part = w_ref[0] * (tile(warm_v, g) + jnp.log(done))
                part_v[0, :, pl.ds(TILE * g, TILE), :] = part[:, :, :128]
                part_v[1, :, pl.ds(TILE * g, TILE), :] = part[:, :, 128:]
                cot = jnp.concatenate(
                    [cot_v[0, :, pl.ds(TILE * g, TILE), :], cot_v[1, :, pl.ds(TILE * g, TILE), :]], axis=2
                )
                u[2, g, own] = (w_ref[0] * cot) / done
                x_start(2, g)
            else:
                grad_v[:, pl.ds(TILE * g, TILE), :] = u[1, g, own] * done
        if turn == 1:
            part_copy = peer_copy(1, part_v.at[1 - inp], peer_v)
            part_copy.start()

    store = pltpu.make_async_copy(grad_v, grad_hbm, out_sem.at[0])
    store.start()
    stores.append(store)
    part_copy.wait_recv()
    bary_v[...] = part_v[inp] + peer_v[...]
    store = pltpu.make_async_copy(bary_v, bary_hbm, out_sem.at[1])
    store.start()
    stores.append(store)

    cot_copy.wait_send()
    part_copy.wait_send()
    for turn in range(3):
        for side in (0, 1):
            if rx:
                @pl.when(has["x", side])
                def _(turn=turn, side=side):
                    for g in range(4):
                        x_copy(turn, g, side).wait_send()
            if ry:
                @pl.when(has["y", side])
                def _(turn=turn, side=side):
                    y_copy(turn, side).wait_send()
    for store in stores:
        store.wait()


def fused(rx, ry, band_reach, weights, warm, log_inputs, cotangent):
    hx = BLOCK * rx
    depth_y = 3 if ry else 1
    groups_y = 6 if ry else 4
    any_space = pl.BlockSpec(memory_space=pl.ANY)
    smem = pl.BlockSpec(memory_space=pltpu.SMEM)
    dma = pltpu.SemaphoreType.DMA
    field = pltpu.VMEM((16, 32, 256), F32)
    half = pltpu.VMEM((16, 32, 128), F32)
    matrix_x = pltpu.VMEM((128, 8 * (16 + 2 * hx)), BF16)
    matrix_y = pltpu.VMEM((64, 64 * depth_y), BF16)
    matrix_z = pltpu.VMEM((256, 256), BF16)
    return pl.pallas_call(
        functools.partial(kernel, rx, ry),
        out_shape=(
            jax.ShapeDtypeStruct((16, 32, 128), F32),
            jax.ShapeDtypeStruct((16, 32, 256), F32),
        ),
        in_specs=[smem, smem, any_space, any_space, any_space],
        out_specs=(any_space, any_space),
        scratch_shapes=[
            field, field,
            pltpu.VMEM((3, 4, 16 + 2 * hx, TILE, 256), F32),
            pltpu.VMEM((3, groups_y, 16, TILE, 256), F32),
            pltpu.VMEM((2, 16, 32, 128), F32),
            pltpu.VMEM((2, 16, 32, 128), F32),
            half, half, field,
            matrix_x, matrix_x, matrix_y, matrix_y, matrix_z, matrix_z,
            dma((3,)), dma((2,)),
            dma((3, 4, 2)), dma((3, 4, 2)), dma((3, 2)), dma((3, 2)), dma((2,)), dma((2,)),
        ],
        compiler_params=pltpu.CompilerParams(
            collective_id=3 * rx + ry, has_side_effects=True, vmem_limit_bytes=40 << 20
        ),
    )(band_reach, weights, warm, log_inputs, cotangent)


def per_device(log_inputs, warm_potential, bary_weights, band_reach, bary_cotangent):
    barycenter, input_grad = fused(
        2, 2, band_reach, bary_weights, warm_potential[0], log_inputs[0], bary_cotangent
    )
    return barycenter, input_grad[None]


def solution(mesh):
    return jax.shard_map(
        per_device,
        mesh=mesh,
        in_specs=(
            P("inp", "pa", "pb", None),
            P("inp", "pa", "pb", None),
            P("inp"),
            P(),
            P("pa", "pb", "inp"),
        ),
        out_specs=(P("pa", "pb", "inp"), P("inp", "pa", "pb", None)),
        check_vma=False,
    )
```

time: 393 us -> 46.9 us (0.12)
  the two profiles are of different devices: /device:TPU:9 before, /device:TPU:227 now
where the time goes in v1:
time: 46.9 us; the launch traced here: 46.7 us
  Pallas kernels  40.2 us (86%)
  local copies, waits for them, and re-layouts  5.18 us (11%)
  between operations  1.3 us (3%)
    pallas_call x1, Pallas kernels, fused(): pl.pallas_call(functools.partial(kernel, rx, ry), out_shape=(jax.ShapeDty...  40.2 us
    unnamed x10, local copies, waits for them, and re-layouts  5.18 us

profile of v1, /device:TPU:227, one launch (start us, length us, event | category | flops | bytes accessed | tf_op | source)
XLA Modules:
  0.0 46.7 jit_solution(2802831783846748551)
XLA Ops:
  1.3 0.0 copy-start.3
  1.3 0.6 %copy-done.3 = s32[3]{0:T(128)S(1)} copy-done((s32[3]{0:T(128)S(1)}, s32[3]{0:T(128)}, u32[]{:S(2)}) %copy-start.3) | copy-done | bytes 36
  1.9 0.0 copy-start
  1.9 1.0 %copy-done = f32[1,16,32,256]{3,2,1,0:T(8,128)S(1)} copy-done((f32[1,16,32,256]{3,2,1,0:T(8,128)S(1)}, f32[1,16,32,256]{3,2,1,0:T(8,128)}, u32[]{:S(2)}) %copy-start) | copy-done | bytes 524312
  3.0 0.0 copy-start.1
  3.0 1.0 %copy-done.1 = f32[1,16,32,256]{3,2,1,0:T(8,128)S(1)} copy-done((f32[1,16,32,256]{3,2,1,0:T(8,128)S(1)}, f32[1,16,32,256]{3,2,1,0:T(8,128)}, u32[]{:S(2)}) %copy-start.1) | copy-done | bytes 524312
  4.0 0.0 copy-start.2
  4.0 0.9 %copy-done.2 = f32[16,32,128]{2,1,0:T(8,128)S(1)} copy-done((f32[16,32,128]{2,1,0:T(8,128)S(1)}, f32[16,32,128]{2,1,0:T(8,128)}, u32[]{:S(2)}) %copy-start.2) | copy-done | bytes 262168
  5.0 40.2 %shard_map.68 = (f32[16,32,128]{2,1,0:T(8,128)S(1)}, f32[16,32,256]{2,1,0:T(8,128)S(1)}) custom-call(s32[3]{0:T(128)S(1)} %copy-done.3, f32[1]{0:T(128)S(6)} %copy.9.w_ref, f32[16,32,256]{2,1,0:T(8,128)S(1)} %bitcast.3, f32[16,32,256]{2,1,0:T(8,128)S(1)} %bitcast.4, f32[16,32,128]{2,1,0:T(8,128)S(1)} %copy-done.2), custom_call_target="tpu_custom_call" | custom-call | tf_op jit(solution)/shard_map/pallas_call | solution.py:266
  45.2 0.7 %copy.10 = f32[16,32,128]{2,1,0:T(8,128)} copy(f32[16,32,128]{2,1,0:T(8,128)S(1)} %get-tuple-element.8) | data formatting | bytes 524288
  45.9 0.8 %copy.11 = f32[1,16,32,256]{3,2,1,0:T(8,128)} copy(f32[1,16,32,256]{3,2,1,0:T(8,128)S(1)} %bitcast.5) | data formatting | bytes 1048576
Async XLA Ops:
  1.3 0.7 %copy-start.3 = (s32[3]{0:T(128)S(1)}, s32[3]{0:T(128)}, u32[]{:S(2)}) copy-start(s32[3]{0:T(128)} %reach_ref.1) | copy-start | bytes 40
  1.9 1.0 %copy-start = (f32[1,16,32,256]{3,2,1,0:T(8,128)S(1)}, f32[1,16,32,256]{3,2,1,0:T(8,128)}, u32[]{:S(2)}) copy-start(f32[1,16,32,256]{3,2,1,0:T(8,128)} %param.6) | copy-start | bytes 1572868
  3.0 1.0 %copy-start.1 = (f32[1,16,32,256]{3,2,1,0:T(8,128)S(1)}, f32[1,16,32,256]{3,2,1,0:T(8,128)}, u32[]{:S(2)}) copy-start(f32[1,16,32,256]{3,2,1,0:T(8,128)} %param.5) | copy-start | bytes 1572868
  4.0 0.9 %copy-start.2 = (f32[16,32,128]{2,1,0:T(8,128)S(1)}, f32[16,32,128]{2,1,0:T(8,128)}, u32[]{:S(2)}) copy-start(f32[16,32,128]{2,1,0:T(8,128)} %cot_hbm.1) | copy-start | bytes 786436

commit v2 on v0

v2 whole, which is shorter than its diff:
```python
import functools
import math

import jax
import jax.numpy as jnp
from jax import lax
from jax.experimental import pallas as pl
from jax.experimental.pallas import tpu as pltpu
from jax.sharding import PartitionSpec as P

MESH = pl.DeviceIdType.MESH
F32 = jnp.float32
BF16 = jnp.bfloat16
BLOCK = 4
SIGMA = 3.0
OUTER, INNER = (0, 3), (1, 2)
CASES = ((0, 1), (0, 2), (1, 0), (1, 2), (2, 0), (2, 1))


def weight(row, column, reach):
    offset = (row - column).astype(F32)
    inside = jnp.abs(row // BLOCK - column // BLOCK) <= reach
    gauss = jnp.exp(-offset * offset / (2.0 * SIGMA * SIGMA)) / (SIGMA * math.sqrt(2.0 * math.pi))
    return 0.5 * jnp.where(row == column, 1.0, 0.0) + 0.5 * jnp.where(inside, gauss, 0.0)


def iotas(rows, columns):
    shape = (rows, columns)
    return lax.broadcasted_iota(jnp.int32, shape, 0), lax.broadcasted_iota(jnp.int32, shape, 1)


def split(value):
    high = value.astype(BF16)
    return high, (value - high.astype(F32)).astype(BF16)


def stacked(value):
    return jnp.concatenate(split(value), axis=0)


def doubled(matrix):
    high, low = split(matrix)
    return jnp.concatenate(
        [jnp.concatenate([high, high], axis=1), jnp.concatenate([low, low], axis=1)], axis=0
    )


def dot(a, b):
    return jnp.dot(a, b, preferred_element_type=F32)


def product(left, parts):
    both = dot(left, parts)
    rows = both.shape[0] // 2
    return both[:rows] + both[rows:]


def kernel(
    rx, ry, w_ref, warm_hbm, log_hbm, cot_hbm, bary_v, grad_v,
    warm_v, log_v, cot_v, own, x_halo, y_out, y_halo, acc_x, acc_y, v_high, v_low,
    part_v, peer_v, mx, mxh, my, myh, kzh, kzl,
    in_sem, x_send, x_recv, y_send, y_recv, i_send, i_recv,
):
    rz = 3 - rx - ry
    hx = BLOCK * rx
    inp, pa, pb = (lax.axis_index(name) for name in ("inp", "pa", "pb"))
    near_x = ({"pa": pa - 1}, {"pa": pa + 1})
    near_y = ({"pb": pb - 1}, {"pb": pb + 1})
    has_x = (pa > 0, pa < lax.axis_size("pa") - 1)
    has_y = (pb > 0, pb < lax.axis_size("pb") - 1)
    partner = {"inp": 1 - inp}

    loads = [
        pltpu.make_async_copy(warm_hbm, warm_v, in_sem.at[0]),
        pltpu.make_async_copy(cot_hbm, cot_v.at[inp], in_sem.at[1]),
        pltpu.make_async_copy(log_hbm, log_v, in_sem.at[2]),
    ]
    for load in loads:
        load.start()

    barrier = pltpu.get_barrier_semaphore()
    pl.semaphore_signal(barrier, inc=1, device_id=partner, device_id_type=MESH)
    others = 1
    for near, has, used in ((near_x, has_x, rx), (near_y, has_y, ry)):
        for side in (0, 1):
            if used:
                @pl.when(has[side])
                def _(device=near[side]):
                    pl.semaphore_signal(barrier, inc=1, device_id=device, device_id_type=MESH)
                others = others + has[side].astype(jnp.int32)

    for side in (0, 1):
        if rx:
            @pl.when(jnp.logical_not(has_x[side]))
            def _(side=side):
                x_halo[:, :, side] = jnp.zeros((3, 4, hx, 8, 256), F32)
        if ry:
            @pl.when(jnp.logical_not(has_y[side]))
            def _(side=side):
                y_halo[:, side] = jnp.zeros((3, *y_halo.shape[2:]), F32)

    if rx:
        row, column = iotas(128, 128)
        lines = weight(row % 8, column % 8, 0) if ry == 0 else (row % 8 == column % 8).astype(F32)
        mx[...] = doubled(lines * weight(row // 8, column // 8, rx))
        row, column = iotas(128, 16 * hx)
        place = jnp.where(column < 8 * hx, column // 8, 16 + column // 8)
        lines = weight(row % 8, column % 8, 0) if ry == 0 else (row % 8 == column % 8).astype(F32)
        mxh[...] = doubled(lines * weight(row // 8 + hx, place, rx))
    if ry:
        def lines_x(row, column):
            return (row == column).astype(F32) if rx else weight(row, column, 0)

        row, column = iotas(128, 128)
        entries = weight(8 * (row // 32) + row % 8, 8 * (column // 32) + column % 8, ry)
        my[...] = doubled(lines_x((row % 32) // 8, (column % 32) // 8) * entries)
    if ry == 2:
        place = jnp.where(column < 64, column % 8, 40 + column % 8)
        entries = weight(8 + 24 * (row // 64) + row % 8, place, ry)
        myh[...] = doubled(lines_x((row % 64) // 8, (column % 64) // 8) * entries)
    if ry == 1:
        row, column = iotas(256, 128)
        place = jnp.where(column < 64, column % 4, 36 + column % 4)
        entries = weight(4 + 24 * (row // 128) + row % 8, place, ry)
        line = 2 * ((column % 64) // 8) + (column % 8) // 4
        myh[...] = doubled(lines_x((row % 128) // 8, line) * entries)
    row, column = iotas(256, 256)
    kzh[...], kzl[...] = split(weight(row, column, rz))

    def tile(ref, g):
        return ref[:, pl.ds(8 * g, 8), :]

    def remote(source, target, send, recv, device):
        return pltpu.make_async_remote_copy(
            src_ref=source, dst_ref=target, send_sem=send, recv_sem=recv,
            device_id=device, device_id_type=MESH,
        )

    def x_copy(turn, g, side):
        return remote(
            own.at[turn, g, pl.ds(0 if side == 0 else 16 - hx, hx)], x_halo.at[turn, g, 1 - side],
            x_send.at[turn, g, side], x_recv.at[turn, g, 1 - side], near_x[side],
        )

    def y_copy(turn, side):
        whole = ry == 2 and rx == 0
        return remote(
            own.at[turn, OUTER[side]] if whole else y_out.at[turn, side], y_halo.at[turn, 1 - side],
            y_send.at[turn, side], y_recv.at[turn, 1 - side], near_y[side],
        )

    def cot_copy(piece, slot):
        rows = pl.ds(8 * piece, 8)
        return remote(
            cot_v.at[slot, rows], cot_v.at[slot, rows], i_send.at[piece], i_recv.at[piece], partner
        )

    def part_copy(g):
        return remote(
            part_v.at[1 - inp, g], peer_v.at[g], i_send.at[2 + g], i_recv.at[2 + g], partner
        )

    def x_start(turn, pair):
        for side in (0, 1):
            @pl.when(has_x[side])
            def _(side=side):
                for g in pair:
                    x_copy(turn, g, side).start()

    def y_start(turn, g, value):
        side = OUTER.index(g)
        if ry == 2 and rx:
            y_out[turn, side] = value
        if ry == 1:
            value = value.reshape(8, 2, 8, 256)
            start = 4 * side
            y_out[turn, side] = jnp.concatenate(
                [value[:, 0, start : start + 4], value[:, 1, start : start + 4]], axis=1
            )

        @pl.when(has_y[side])
        def _():
            y_copy(turn, side).start()

    def enter(turn, pair):
        if rx:
            x_start(turn, pair)
        else:
            for g in pair:
                if g in OUTER:
                    y_start(turn, g, own[turn, g])

    def own_part(turn, pair):
        for g in pair:
            value = own[turn, g].reshape(128, 256)
            if rx:
                acc_x[g] = product(mx[...], stacked(value))
            else:
                v_high[g], v_low[g] = split(value)

    def x_finish(turn, pair):
        for side in (0, 1):
            @pl.when(has_x[side])
            def _(side=side):
                for g in pair:
                    x_copy(turn, g, 1 - side).wait_recv()
        totals = []
        for g in pair:
            halo = x_halo[turn, g].reshape(16 * hx, 256)
            totals.append(acc_x[g] + product(mxh[...], stacked(halo)))
        return totals

    def y_own():
        for q in range(4):
            rows = pl.ds(32 * q, 32)
            parts = jnp.concatenate(
                [v_high[:, rows].reshape(128, 256), v_low[:, rows].reshape(128, 256)], axis=0
            )
            acc_y[:, rows] = product(my[...], parts).reshape(4, 32, 256)

    def y_finish(turn):
        for side in (0, 1):
            @pl.when(has_y[side])
            def _(side=side):
                y_copy(turn, 1 - side).wait_recv()
        if ry == 2:
            pieces = []
            for half in (0, 1):
                halo = y_halo[turn, :, pl.ds(8 * half, 8)].reshape(128, 256)
                pieces.append(product(myh[...], stacked(halo)))
            more = [jnp.concatenate([p[64 * e : 64 * e + 64] for p in pieces], axis=0) for e in (0, 1)]
        else:
            both = product(myh[...], stacked(y_halo[turn].reshape(128, 256)))
            more = [both[:128], both[128:]]
        return [acc_y[g] + extra for g, extra in zip(OUTER, more)]

    def epilogue(turn, pair, totals):
        high, low = split(jnp.concatenate(totals, axis=0))
        both = dot(jnp.concatenate([high, low], axis=0), kzh[...])
        both = both[:256] + both[256:] + dot(high, kzl[...])
        done = [both[:128].reshape(16, 8, 256), both[128:].reshape(16, 8, 256)]
        for g, value in zip(pair, done):
            if turn == 0:
                own[1, g] = jnp.exp(tile(log_v, g)) / value
            elif turn == 1:
                cot = jnp.concatenate([tile(cot_v.at[0], g), tile(cot_v.at[1], g)], axis=2)
                own[2, g] = (w_ref[0] * cot) / value
            else:
                grad_v[:, pl.ds(8 * g, 8), :] = own[1, g] * value
        if turn == 2:
            return
        enter(turn + 1, pair)
        if turn == 1:
            for g, value in zip(pair, done):
                part = w_ref[0] * (tile(warm_v, g) + jnp.log(value))
                part_v[0, g] = part[:, :, :128]
                part_v[1, g] = part[:, :, 128:]
        own_part(turn + 1, pair)

    loads[0].wait()
    for g in OUTER + INNER:
        own[0, g] = jnp.exp(tile(warm_v, g))
    loads[1].wait()
    pl.semaphore_wait(barrier, others)

    first, second = (OUTER, INNER) if rx == 2 or ry == 0 else (INNER, OUTER)

    enter(0, OUTER)
    if rx:
        enter(0, INNER)
    cot_copy(0, inp).start()
    if rx < 2:
        cot_copy(1, inp).start()
    own_part(0, OUTER)
    own_part(0, INNER)
    loads[2].wait()

    for turn in range(3):
        if rx and ry:
            for pair in (OUTER, INNER) if turn == 0 else (first, second):
                for g, total in zip(pair, x_finish(turn, pair)):
                    v_high[g], v_low[g] = split(total)
                    if g in OUTER:
                        y_start(turn, g, total.reshape(16, 8, 256))
        if ry:
            y_own()
        if turn == 1:
            for piece in (0, 1):
                cot_copy(piece, 1 - inp).wait_recv()
        for pair in (first, second):
            if ry == 0:
                totals = x_finish(turn, pair)
            elif pair == OUTER:
                totals = y_finish(turn)
            else:
                totals = [acc_y[g] for g in pair]
            epilogue(turn, pair, totals)
            if turn == 1 and rx == 0:
                for g in pair:
                    part_copy(g).start()
        if turn == 0 and rx == 2:
            cot_copy(1, inp).start()
        if turn == 1 and rx:
            for g in first + second:
                part_copy(g).start()

    for g in first + second:
        part_copy(g).wait_recv()
        bary_v[:, pl.ds(8 * g, 8), :] = part_v[inp, g] + peer_v[g]

    for piece in (0, 1):
        cot_copy(piece, inp).wait_send()
    for g in range(4):
        part_copy(g).wait_send()
    for side in (0, 1):
        if rx:
            @pl.when(has_x[side])
            def _(side=side):
                for turn in range(3):
                    for g in range(4):
                        x_copy(turn, g, side).wait_send()
        if ry:
            @pl.when(has_y[side])
            def _(side=side):
                for turn in range(3):
                    y_copy(turn, side).wait_send()


def fused(rx, ry, weights, warm, log_inputs, cotangent):
    hx = BLOCK * rx
    hbm = pl.BlockSpec(memory_space=pltpu.HBM)
    smem = pl.BlockSpec(memory_space=pltpu.SMEM)
    vmem = pl.BlockSpec(memory_space=pltpu.VMEM)
    dma = pltpu.SemaphoreType.DMA
    field = pltpu.VMEM((16, 32, 256), F32)
    halves = pltpu.VMEM((2, 16, 32, 128), F32)
    rows_y = 16 if ry == 2 else 8
    matrix = pltpu.VMEM((256, 256), BF16)
    return pl.pallas_call(
        functools.partial(kernel, rx, ry),
        out_shape=(
            jax.ShapeDtypeStruct((16, 32, 128), F32),
            jax.ShapeDtypeStruct((16, 32, 256), F32),
        ),
        in_specs=[smem, hbm, hbm, hbm],
        out_specs=(vmem, vmem),
        scratch_shapes=[
            field, field, halves,
            pltpu.VMEM((3, 4, 16, 8, 256), F32),
            pltpu.VMEM((3, 4, 2, max(hx, 1), 8, 256), F32),
            pltpu.VMEM((3, 2, rows_y, 8, 256), F32),
            pltpu.VMEM((3, 2, rows_y, 8, 256), F32),
            pltpu.VMEM((4, 128, 256), F32),
            pltpu.VMEM((4, 128, 256), F32),
            pltpu.VMEM((4, 128, 256), BF16),
            pltpu.VMEM((4, 128, 256), BF16),
            pltpu.VMEM((2, 4, 16, 8, 128), F32),
            pltpu.VMEM((4, 16, 8, 128), F32),
            matrix,
            pltpu.VMEM((256, 32 * max(hx, 4)), BF16),
            matrix,
            pltpu.VMEM((512 if ry == 1 else 256, 256), BF16),
            matrix, matrix,
            dma((3,)), dma((3, 4, 2)), dma((3, 4, 2)), dma((3, 2)), dma((3, 2)), dma((6,)), dma((6,)),
        ],
        compiler_params=pltpu.CompilerParams(
            collective_id=3 * rx + ry, has_side_effects=True, vmem_limit_bytes=40 << 20
        ),
    )(weights, warm, log_inputs, cotangent)


def store(bary_v, grad_v, bary_hbm, grad_hbm, sems):
    copies = [
        pltpu.make_async_copy(bary_v, bary_hbm, sems.at[0]),
        pltpu.make_async_copy(grad_v, grad_hbm, sems.at[1]),
    ]
    for copy in copies:
        copy.start()
    for copy in copies:
        copy.wait()


def stored(bary, grad):
    vmem = pl.BlockSpec(memory_space=pltpu.VMEM)
    hbm = pl.BlockSpec(memory_space=pltpu.HBM)
    return pl.pallas_call(
        store,
        out_shape=(
            jax.ShapeDtypeStruct(bary.shape, F32),
            jax.ShapeDtypeStruct(grad.shape, F32),
        ),
        in_specs=[vmem, vmem],
        out_specs=(hbm, hbm),
        scratch_shapes=[pltpu.SemaphoreType.DMA((2,))],
    )(bary, grad)


def choose(reach_ref, index_ref):
    index_ref[0] = 2 * reach_ref[0] + (reach_ref[1] > reach_ref[2]).astype(jnp.int32)


def per_device(log_inputs, warm_potential, bary_weights, band_reach, bary_cotangent):
    index = pl.pallas_call(
        choose,
        out_shape=jax.ShapeDtypeStruct((1,), jnp.int32),
        in_specs=[pl.BlockSpec(memory_space=pltpu.SMEM)],
        out_specs=pl.BlockSpec(memory_space=pltpu.SMEM),
    )(band_reach)[0]
    branches = [functools.partial(fused, rx, ry) for rx, ry in CASES]
    bary, grad = lax.switch(
        index, branches, bary_weights, warm_potential[0], log_inputs[0], bary_cotangent
    )
    bary, grad = stored(bary, grad)
    return bary, grad[None]


def solution(mesh):
    return jax.shard_map(
        per_device,
        mesh=mesh,
        in_specs=(
            P("inp", "pa", "pb", None),
            P("inp", "pa", "pb", None),
            P("inp"),
            P(),
            P("pa", "pb", "inp"),
        ),
        out_specs=(P("pa", "pb", "inp"), P("inp", "pa", "pb", None)),
        check_vma=False,
    )
```

time: 393 us -> 24.4 us (0.06)
  the two profiles are of different devices: /device:TPU:9 before, /device:TPU:36 now
where the time goes in v2:
time: 24.4 us; the launch traced here: 24.2 us
  Pallas kernels  22.5 us (92%)
  between operations  1.47 us (6%)
  loops' own time  0.25 us (1%)
    pallas_call x1, Pallas kernels, fused(): pl.pallas_call(functools.partial(kernel, rx, ry), out_shape=(jax.ShapeDty...  20.4 us
    pallas_call x1, Pallas kernels, per_device(): pl.pallas_call(choose, out_shape=jax.ShapeDtypeStruct((1,), jnp.int32), i...  1.18 us
    pallas_call x1, Pallas kernels, stored(): pl.pallas_call(store, out_shape=(jax.ShapeDtypeStruct(bary.shape, F32), j...  0.9 us

profile of v2, /device:TPU:36, one launch (start us, length us, event | category | flops | bytes accessed | tf_op | source)
XLA Modules:
  0.0 24.2 jit_solution(6266224388470090371)
XLA Ops:
  0.6 1.2 %shard_map.68 = s32[1]{0:T(128)} custom-call(s32[3]{0:T(128)} %reach_ref.1), custom_call_target="tpu_custom_call" | custom-call | tf_op jit(solution)/shard_map/pallas_call | solution.py:403
  2.5 20.7 %conditional.1 = ((f32[16,32,128]{2,1,0:T(8,128)S(1)}, f32[16,32,256]{2,1,0:T(8,128)S(1)})) conditional(s32[]{:T(128)} %bitcast, (f32[1]{0:T(128)}, f32[16,32,256]{2,1,0:T(8,128)}, f32[16,32,256]{2,1,0:T(8,128)}, f32[16,32,128]{2,1,0:T(8,128)}) %tuple.46, (f32[1]{0:T(128)}, f32[16,32,256]{2,1,0:T(8,128)}, ...), branch_computations={%region_0.0_spmd, %region_1.0_spmd, %region_2.0_spmd, %region_3.0_... | conditional | bytes 8 | solution.py:410
  2.5 20.4 %branch_0_fun.1 = (f32[16,32,128]{2,1,0:T(8,128)S(1)}, f32[16,32,256]{2,1,0:T(8,128)S(1)}) custom-call(f32[1]{0:T(128)} %get-tuple-element.48.w_ref, f32[16,32,256]{2,1,0:T(8,128)} %get-tuple-element.49.warm_hbm, f32[16,32,256]{2,1,0:T(8,128)} %get-tuple-element.50.log_hbm, f32[16,32,128]{2,1,0:T(8,128)} %get-tuple-element.51.cot_hbm), custom_call_target="tpu_custom_call" | custom-call | tf_op jit(solution)/shard_map/cond/branch_0_fun/pallas_call | solution.py:339
  23.1 0.9 %shard_map.69 = (f32[16,32,128]{2,1,0:T(8,128)}, f32[16,32,256]{2,1,0:T(8,128)}) custom-call(f32[16,32,128]{2,1,0:T(8,128)S(1)} %get-tuple-element.78.bary_v, f32[16,32,256]{2,1,0:T(8,128)S(1)} %get-tuple-element.79.grad_v), custom_call_target="tpu_custom_call" | custom-call | tf_op jit(solution)/shard_map/pallas_call | solution.py:386
